TPU v7x, 32 devices: a whole 2x2x4 slice. The times are simulated.
32 devices in a mesh: grp: 8 (over y, x, core), leaf: 4 (over z).
Axes of the slice: x: 2, y: 2, z: 4, core: 2. Of those that a mesh axis runs over, the one named last changes fastest.
Arguments:
- labels: int32 [16384], P(('grp', 'leaf')), may hold values from 0 to 255
- leaf_inverse: float32 [16384, 512], P(('grp', 'leaf')), may hold values from -1 to 4
- leaf_basis: float32 [16384, 128], P(('grp', 'leaf')), may hold values from -0.25 to 0.25
- leaf_solved: float32 [16384, 128], P(('grp', 'leaf')), may hold values from -0.5 to 0.5
- group_capacitance: float32 [4096, 512], P(('grp', 'leaf')), may hold values from -1 to 4
- top_basis: float32 [16384, 128], P(('grp', 'leaf')), may hold values from -0.125 to 0.125
- top_solved: float32 [16384, 128], P(('grp', 'leaf')), may hold values from -0.5 to 0.5
- top_capacitance: float32 [1024, 1024], P('grp'), may hold values from -1 to 4
Outputs:
- dual_box: float32 [16384, 256], P(('grp', 'leaf'))
- scaled_dual: float32 [16384, 256], P(('grp', 'leaf'))
All inputs are finite; a program needn't handle non-finite values.
Results may differ from a plain program's by a relative error of at most 0.0003.
Values sent between devices are 32-bit elements; how exact they have to be, the bound alone decides.
A program may use at most 64 MiB of HBM per device.

v0:
```python
import jax
import jax.numpy as jnp
from jax import lax
from jax.sharding import PartitionSpec as P

CLASSES = 256
ITERS = 2


high = lax.Precision.HIGHEST


def matmul(left, right):
    return jnp.dot(left, right, precision=high, preferred_element_type=jnp.float32)


def project_rows(basis, values):
    return lax.dot_general(
        basis, values, (((0,), (0,)), ((), ())), precision=high, preferred_element_type=jnp.float32
    )


def column_product(matrix, piece):
    return matmul(matrix, piece)


def shards(
    labels,
    leaf_inverse,
    leaf_basis,
    leaf_solved,
    group_capacitance,
    top_basis,
    top_solved,
    top_capacitance,
):
    columns = lax.broadcasted_iota(jnp.int32, (labels.shape[0], CLASSES), 1)
    label_sign = jnp.where(labels[:, None] == columns, 1.0, -1.0).astype(jnp.float32)
    dual_box = jnp.zeros((labels.shape[0], CLASSES), jnp.float32)
    scaled_dual = jnp.zeros((labels.shape[0], CLASSES), jnp.float32)
    for iteration in range(ITERS):
        rhs = label_sign * (1.0 + 1.0 * (dual_box - scaled_dual))
        local = matmul(leaf_inverse, rhs)
        coeffs = project_rows(leaf_basis, local)
        group_coef = column_product(
            group_capacitance, lax.all_gather(coeffs, "leaf", axis=0, tiled=True)
        )
        inner = local - matmul(leaf_solved, group_coef)
        partial_proj = project_rows(top_basis, inner)
        share = lax.psum_scatter(partial_proj, "leaf", scatter_dimension=1, tiled=True)
        share_coef = column_product(
            top_capacitance, lax.all_gather(share, "grp", axis=0, tiled=True)
        )
        top_coef = lax.all_gather(share_coef, "leaf", axis=1, tiled=True)
        solved = inner - matmul(top_solved, top_coef)
        moved = scaled_dual + label_sign * solved
        dual_box = jnp.clip(moved, 0.0, 1.0)
        scaled_dual = moved - dual_box
    return (dual_box, scaled_dual)


def solution(mesh):
    return jax.shard_map(
        shards,
        mesh=mesh,
        in_specs=(
            P(("grp", "leaf")),
            P(("grp", "leaf"), None),
            P(("grp", "leaf"), None),
            P(("grp", "leaf"), None),
            P(("grp", "leaf"), None),
            P(("grp", "leaf"), None),
            P(("grp", "leaf"), None),
            P("grp", None),
        ),
        out_specs=(P(("grp", "leaf"), None), P(("grp", "leaf"), None)),
        check_vma=False,
    )
```

profile of v0, /device:TPU:0, one launch (start us, length us, event | category | flops | bytes accessed | tf_op | source)
XLA Modules:
  0.0 148.3 jit_solution(11948927339360543717)
XLA Ops:
  7.2 0.0 copy-start
  7.2 0.0 copy-start.2
  7.2 0.0 reduce-scatter.3.cloned.1.call-start
  7.2 1.2 copy-done
  8.4 1.8 %fusion.5 = f32[256,512]{1,0:T(8,128)S(1)} fusion(f32[512,512]{1,0:T(8,128)S(1)} %copy-done, s32[512]{0:T(512)} %param.8), kind=kOutput, calls=%fused_computation.16 | convolution fusion | flops 805568512 | bytes 1574912 | tf_op jit(solution)/shard_map/dot_general | solution.py:14
  10.2 0.0 copy-done.2
  10.2 0.6 convolution_bitcast_fusion.3
  10.8 0.0 copy-start.3
  10.8 17.5 %all_gather.18 = f32[512,256]{0,1:T(8,128)S(1)} all-gather(f32[128,256]{0,1:T(8,128)S(1)} %convolution_bitcast_fusion.3), channel_id=1, replica_groups=mesh['grp'=8,'leaf'=4] {'leaf'}, dimensions={0}, use_global_device_ids=true | all-gather | bytes 655360 | tf_op jit(solution)/shard_map/all_gather | solution.py:46
  28.3 0.0 copy-done.3
  28.3 0.0 copy-start.5
  28.3 0.6 fusion.22
  28.9 0.4 copy-done.5
  29.2 0.0 copy-start.4
  29.2 0.6 convolution_subtract_fusion.3
  29.8 0.4 copy-done.4
  30.2 0.0 copy-start.1
  30.2 1.2 convolution_bitcast_fusion.2
  31.4 0.0 reduce-scatter.3.cloned.1.call-update
  31.5 0.0 reduce-scatter.5.cloned.1.call-start
  31.5 21.3 %reduce-scatter.3.cloned.1.call-done = f32[128,64]{0,1:T(8,128)} async-done(((f32[128,256]{0,1:T(8,128)}), f32[128,64]{0,1:T(8,128)}) %reduce-scatter.3.cloned.1.call-update) | async-done | bytes 32784 | tf_op jit(solution)/shard_map/reduce_scatter | solution.py:50
  52.8 10.0 %all_gather.19 = f32[1024,64]{0,1:T(8,128)S(1)} all-gather(f32[128,64]{0,1:T(8,128)} %reduce-scatter.3.cloned.1.call-done), channel_id=1, replica_groups=mesh['grp'=8,'leaf'=4] {'grp'}, dimensions={0}, use_global_device_ids=true | all-gather | bytes 294912 | tf_op jit(solution)/shard_map/all_gather | solution.py:52
  62.8 0.0 copy-done.1
  62.8 0.0 copy-start.7
  62.8 0.7 convolution_bitcast_fusion.5
  63.5 0.0 copy-start.9
  63.5 13.5 %all_gather.20 = f32[128,256]{0,1:T(8,128)S(1)} all-gather(f32[128,64]{0,1:T(8,128)S(1)} %convolution_bitcast_fusion.5), channel_id=1, replica_groups=mesh['grp'=8,'leaf'=4] {'leaf'}, dimensions={1}, use_global_device_ids=true | all-gather | bytes 163840 | tf_op jit(solution)/shard_map/all_gather | solution.py:54
  77.0 0.0 copy-done.7
  77.0 0.0 copy-done.9
  77.0 0.6 fusion.4
  77.6 1.2 fusion.8
  78.8 0.6 convolution_bitcast_fusion.1
  79.4 14.8 %all_gather.21 = f32[512,256]{0,1:T(8,128)S(1)} all-gather(f32[128,256]{0,1:T(8,128)S(1)} %convolution_bitcast_fusion.1), channel_id=1, replica_groups=mesh['grp'=8,'leaf'=4] {'leaf'}, dimensions={0}, use_global_device_ids=true | all-gather | bytes 655360 | tf_op jit(solution)/shard_map/all_gather | solution.py:46
  94.1 0.0 copy-start.6
  94.1 0.6 fusion.23
  94.7 0.4 copy-done.6
  95.1 0.6 convolution_subtract_fusion.1
  95.7 1.2 convolution_bitcast_fusion
  96.9 0.0 reduce-scatter.5.cloned.1.call-update
  96.9 17.6 %reduce-scatter.5.cloned.1.call-done = f32[128,64]{0,1:T(8,128)} async-done(((f32[128,256]{0,1:T(8,128)}), f32[128,64]{0,1:T(8,128)}) %reduce-scatter.5.cloned.1.call-update) | async-done | bytes 32784 | tf_op jit(solution)/shard_map/reduce_scatter | solution.py:50
  114.5 10.0 %all_gather.22 = f32[1024,64]{0,1:T(8,128)S(1)} all-gather(f32[128,64]{0,1:T(8,128)} %reduce-scatter.5.cloned.1.call-done), channel_id=1, replica_groups=mesh['grp'=8,'leaf'=4] {'grp'}, dimensions={0}, use_global_device_ids=true | all-gather | bytes 294912 | tf_op jit(solution)/shard_map/all_gather | solution.py:52
  124.5 0.0 copy-start.8
  124.5 0.7 convolution_bitcast_fusion.4
  125.2 13.6 %all_gather.23 = f32[128,256]{0,1:T(8,128)S(1)} all-gather(f32[128,64]{0,1:T(8,128)S(1)} %convolution_bitcast_fusion.4), channel_id=1, replica_groups=mesh['grp'=8,'leaf'=4] {'leaf'}, dimensions={1}, use_global_device_ids=true | all-gather | bytes 163840 | tf_op jit(solution)/shard_map/all_gather | solution.py:54
  138.8 0.0 copy-done.8
  138.8 0.7 fusion.16
  139.5 1.0 copy.11
  140.5 1.0 copy.10
Async XLA Ops:
  7.2 1.2 copy-start
  7.2 3.0 %copy-start.2 = (f32[512,128]{1,0:T(8,128)S(1)}, f32[512,128]{1,0:T(8,128)}, u32[]{:S(2)}) copy-start(f32[512,128]{1,0:T(8,128)} %param.10) | copy-start | bytes 786436
  7.2 45.6 %reduce-scatter.3.cloned.1.call-start = ((), (), s32[]{:S(2)}) async-start(), calls=%async_computation.2 | async-start | bytes 163840 | tf_op jit(solution)/shard_map/reduce_scatter | solution.py:50
  10.8 17.5 %copy-start.3 = (f32[128,512]{1,0:T(8,128)S(1)}, f32[128,512]{1,0:T(8,128)}, u32[]{:S(2)}) copy-start(f32[128,512]{1,0:T(8,128)} %param.12) | copy-start | bytes 786436
  28.3 1.0 copy-start.5
  29.2 0.9 copy-start.4
  30.2 32.6 %copy-start.1 = (f32[128,1024]{1,0:T(8,128)S(1)}, f32[128,1024]{1,0:T(8,128)}, u32[]{:S(2)}) copy-start(f32[128,1024]{1,0:T(8,128)} %param.15) | copy-start | bytes 1572868
  31.5 83.1 %reduce-scatter.5.cloned.1.call-start = ((), (), s32[]{:S(2)}) async-start(), calls=%async_computation.3 | async-start | bytes 163840 | tf_op jit(solution)/shard_map/reduce_scatter | solution.py:50
  62.8 14.1 %copy-start.7 = (f32[512,128]{1,0:T(8,128)S(1)}, f32[512,128]{1,0:T(8,128)}, u32[]{:S(2)}) copy-start(f32[512,128]{1,0:T(8,128)} %param.14) | copy-start | bytes 786436
  63.5 13.5 %copy-start.9 = (s32[512]{0:T(512)S(1)}, s32[512]{0:T(512)}, u32[]{:S(2)}) copy-start(s32[512]{0:T(512)} %param.8) | copy-start | bytes 6148
  94.1 1.0 copy-start.6
  124.5 14.3 %copy-start.8 = (f32[512,128]{1,0:T(8,128)S(1)}, f32[512,128]{1,0:T(8,128)}, u32[]{:S(2)}) copy-start(f32[512,128]{1,0:T(8,128)} %param.14) | copy-start | bytes 786436
Sparse Core Ops, SparseCore 0:
  31.6 21.1 reduce-scatter.2
  97.1 17.4 reduce-scatter.4
where the time goes:
time: 149 us; the launch traced here: 148 us
  blocking collectives  79.3 us (53%)
  waiting for transfers between devices  38.9 us (26%)
  between operations  14.2 us (10%)
  matrix products  11.5 us (8%)
  local copies, waits for them, and re-layouts  4.27 us (3%)
    reduce_scatter x2, waiting for transfers between devices, shards(): lax.psum_scatter(partial_proj, 'leaf', scatter_dimension=1, tiled=True)  38.9 us
    all_gather x2, blocking collectives, shards(): lax.all_gather(coeffs, 'leaf', axis=0, tiled=True)  32.3 us
    all_gather x2, blocking collectives, shards(): top_coef = lax.all_gather(share_coef, 'leaf', axis=1, tiled=True)  27.1 us
    all_gather x2, blocking collectives, shards(): lax.all_gather(share, 'grp', axis=0, tiled=True)  20 us
    dot_general x10, matrix products, matmul(): jnp.dot(left, right, precision=high, preferred_element_type=jnp.float32)  7.88 us
    unnamed x22, local copies, waits for them, and re-layouts  4.27 us
    dot_general x4, matrix products, project_rows(): lax.dot_general(basis, values, (((0,), (0,)), ((), ())), precision=high,...  3.65 us
  transfers between devices with their start and end apart: 2, of which 2 were waited for; matrix products, arithmetic and copies ran while one was open for 0% of the time, Pallas kernels for 0%

commit v1 on v0

v1 whole, which is shorter than its diff:
```python
import functools

import jax
import jax.numpy as jnp
from jax import lax
from jax.experimental import pallas as pl
from jax.experimental.pallas import tpu as pltpu
from jax.sharding import PartitionSpec as P

CLASSES = 256
ITERS = 2
NN = (((1,), (0,)), ((), ()))
NT = (((1,), (1,)), ((), ()))


def split(x):
    high = x.astype(jnp.bfloat16)
    low = (x - high.astype(jnp.float32)).astype(jnp.bfloat16)
    return high, low


def dot(a, b, dims):
    return lax.dot_general(a, b, dims, preferred_element_type=jnp.float32)


def product(a, b, dims=NN):
    return dot(a[0], b[0], dims) + (dot(a[0], b[1], dims) + dot(a[1], b[0], dims))


def kernel(
    n,
    m,
    labels_ref,
    inverse_hbm,
    basis_hbm,
    solved_hbm,
    capacitance_hbm,
    top_basis_hbm,
    top_solved_hbm,
    top_capacitance_hbm,
    moved_ref,
    inverse_ref,
    basis_ref,
    solved_ref,
    capacitance_ref,
    top_basis_ref,
    top_solved_ref,
    top_capacitance_ref,
    w_out,
    w_in,
    c_all,
    p_out,
    p_in,
    proj,
    t_all,
    in_sem,
    w_send,
    w_recv,
    c_send,
    c_recv,
    p_send,
    p_recv,
    g_send,
    g_recv,
    t_send,
    t_recv,
):
    me = lax.axis_index("leaf")
    grp = lax.axis_index("grp")
    rows = labels_ref.shape[1]
    rank = basis_ref.shape[1]
    top_rank = top_basis_ref.shape[1]
    share = CLASSES // n

    sources = (
        (top_basis_hbm, top_basis_ref),
        (solved_hbm, solved_ref),
        (capacitance_hbm, capacitance_ref),
        (inverse_hbm, inverse_ref),
        (basis_hbm, basis_ref),
        (top_solved_hbm, top_solved_ref),
        (top_capacitance_hbm, top_capacitance_ref),
    )
    loads = [pltpu.make_async_copy(a, b, in_sem.at[i]) for i, (a, b) in enumerate(sources)]
    for load in loads:
        load.start()

    barrier = pltpu.get_barrier_semaphore()
    for d in range(1, n):
        pl.semaphore_signal(
            barrier, inc=1, device_id={"leaf": lax.rem(me + d, n)},
            device_id_type=pl.DeviceIdType.MESH,
        )
    for d in range(1, m):
        pl.semaphore_signal(
            barrier, inc=1, device_id={"grp": lax.rem(grp + d, m)},
            device_id_type=pl.DeviceIdType.MESH,
        )

    def remote(src, dst, send, recv, where):
        return pltpu.make_async_remote_copy(
            src_ref=src, dst_ref=dst, send_sem=send, recv_sem=recv,
            device_id=where, device_id_type=pl.DeviceIdType.MESH,
        )

    sent = []

    loads[0].wait()
    loads[1].wait()
    loads[2].wait()
    top_basis_t = top_basis_ref[...].T
    solved = split(solved_ref[...])
    capacitance = split(capacitance_ref[...])
    coupling = product(split(product(split(top_basis_t), solved)), capacitance)
    for d in range(n):
        w_out[d] = coupling[:, d * rank : (d + 1) * rank]
    pl.semaphore_wait(barrier, n - 1 + m - 1)
    for d in range(1, n):
        dest = lax.rem(me + d, n)
        copy = remote(w_out.at[dest], w_in.at[d], w_send.at[d], w_recv.at[d], {"leaf": dest})
        copy.start()
        sent.append((None, copy))

    pieces = []
    for r in range(rows // 128):
        row = labels_ref[:, r * 128 : (r + 1) * 128].astype(jnp.float32)
        column = jnp.broadcast_to(row, (128, 128)).T
        lanes = lax.broadcasted_iota(jnp.int32, (128, 128), 1)
        pieces.append(
            jnp.concatenate(
                [
                    jnp.where(column == (lanes + k * 128).astype(jnp.float32), 1.0, -1.0)
                    for k in range(CLASSES // 128)
                ],
                axis=1,
            )
        )
    sign = jnp.concatenate(pieces, axis=0)

    loads[3].wait()
    inverse = split(inverse_ref[...])
    exact = sign.astype(jnp.bfloat16)
    local = dot(inverse[0], exact, NN) + dot(inverse[1], exact, NN)

    loads[4].wait()
    loads[5].wait()
    loads[6].wait()
    top_solved = split(top_solved_ref[...])
    top_capacitance = split(top_capacitance_ref[...])
    basis = basis_ref[...]
    w_sum = w_out[me]
    for d in range(1, n):
        remote(w_out.at[0], w_in.at[d], w_send.at[d], w_recv.at[d], {"leaf": me}).wait_recv()
        w_sum = w_sum + w_in[d]
    combined = top_basis_t - product(split(w_sum), split(basis), NT)
    projector = split(jnp.concatenate([basis.T, combined], axis=0))

    scaled_dual = None
    for it in range(ITERS):
        if it:
            rhs = sign * (1.0 + 1.0 * (dual_box - scaled_dual))
            local = product(inverse, split(rhs))
        both = product(projector, split(local))
        p_out[it] = both[rank:, :].T
        for d in range(1, n):
            dest = lax.rem(me + d, n)
            copy = remote(
                p_out.at[it, pl.ds(pl.multiple_of(dest * share, 8), share)],
                p_in.at[it, d], p_send.at[it, d], p_recv.at[it, d], {"leaf": dest},
            )
            copy.start()
            sent.append((None, copy))
        c_all[it, me] = both[:rank, :]

        def step(k, it=it):
            left, right = jnp.maximum(me - k, 0), jnp.minimum(me + k, n - 1)
            has_left, has_right = me - k >= 0, me + k <= n - 1
            for side, src, has, more, dest in (
                (0, left, has_left, me < n - 1, jnp.minimum(me + 1, n - 1)),
                (1, right, has_right, me > 0, jnp.maximum(me - 1, 0)),
            ):
                if k:
                    @pl.when(has)
                    def _(src=src, side=side):
                        remote(
                            c_all.at[it, src], c_all.at[it, src], c_send.at[it, side, k],
                            c_recv.at[it, side, k], {"leaf": me},
                        ).wait_recv()
                if k < n - 1:
                    copy = remote(
                        c_all.at[it, src], c_all.at[it, src], c_send.at[it, side, k],
                        c_recv.at[it, side, k + 1], {"leaf": dest},
                    )

                    @pl.when(has & more)
                    def _(copy=copy):
                        copy.start()

                    sent.append((has & more, copy))

        step(0)

        total = p_out[it, pl.ds(pl.multiple_of(me * share, 8), share)]
        for d in range(1, n):
            remote(
                p_in.at[it, 0], p_in.at[it, d], p_send.at[it, d], p_recv.at[it, d], {"leaf": me}
            ).wait_recv()
            total = total + p_in[it, d]
        proj[it, grp] = total
        for d in range(1, m):
            copy = remote(
                proj.at[it, grp], proj.at[it, grp], g_send.at[it, d], g_recv.at[it, d],
                {"grp": lax.rem(grp + d, m)},
            )
            copy.start()
            sent.append((None, copy))
        step(1)
        for d in range(1, m):
            src = lax.rem(grp + m - d, m)
            remote(
                proj.at[it, src], proj.at[it, src], g_send.at[it, d], g_recv.at[it, d],
                {"grp": grp},
            ).wait_recv()
        stacked = jnp.concatenate([proj[it, g] for g in range(m)], axis=1)
        mine = pl.ds(pl.multiple_of(me * share, 8), share)
        t_all[it, mine] = product(split(stacked), top_capacitance, NT)
        for d in range(1, n):
            copy = remote(
                t_all.at[it, mine], t_all.at[it, mine], t_send.at[it, d], t_recv.at[it, d],
                {"leaf": lax.rem(me + d, n)},
            )
            copy.start()
            sent.append((None, copy))
        for k in range(2, n):
            step(k)
        coeffs = jnp.concatenate([c_all[it, k] for k in range(n)], axis=0)
        group_coef = product(capacitance, split(coeffs))
        inner = local - product(solved, split(group_coef))
        for d in range(1, n):
            src = pl.ds(pl.multiple_of(lax.rem(me + n - d, n) * share, 8), share)
            remote(
                t_all.at[it, src], t_all.at[it, src], t_send.at[it, d], t_recv.at[it, d],
                {"leaf": me},
            ).wait_recv()
        answer = inner - product(top_solved, split(t_all[it]), NT)
        moved = sign * answer
        if it:
            moved = scaled_dual + moved
        if it < ITERS - 1:
            dual_box = jnp.clip(moved, 0.0, 1.0)
            scaled_dual = moved - dual_box
    moved_ref[...] = moved
    for has, copy in sent:
        if has is None:
            copy.wait_send()
        else:
            @pl.when(has)
            def _(copy=copy):
                copy.wait_send()


def shards(
    n,
    m,
    labels,
    leaf_inverse,
    leaf_basis,
    leaf_solved,
    group_capacitance,
    top_basis,
    top_solved,
    top_capacitance,
):
    rows = labels.shape[0]
    rank = leaf_basis.shape[1]
    top_rank = top_basis.shape[1]
    share = CLASSES // n
    arrays = (
        leaf_inverse,
        leaf_basis,
        leaf_solved,
        group_capacitance,
        top_basis,
        top_solved,
        top_capacitance,
    )
    f32 = jnp.float32
    sem = pltpu.SemaphoreType.DMA
    moved = pl.pallas_call(
        functools.partial(kernel, n, m),
        out_shape=jax.ShapeDtypeStruct((rows, CLASSES), f32),
        in_specs=[pl.BlockSpec(memory_space=pltpu.VMEM)]
        + [pl.BlockSpec(memory_space=pl.ANY)] * len(arrays),
        out_specs=pl.BlockSpec(memory_space=pltpu.VMEM),
        scratch_shapes=[pltpu.VMEM(a.shape, f32) for a in arrays]
        + [
            pltpu.VMEM((n, top_rank, rank), f32),
            pltpu.VMEM((n, top_rank, rank), f32),
            pltpu.VMEM((ITERS, n, rank, CLASSES), f32),
            pltpu.VMEM((ITERS, CLASSES, top_rank), f32),
            pltpu.VMEM((ITERS, n, share, top_rank), f32),
            pltpu.VMEM((ITERS, m, share, top_rank), f32),
            pltpu.VMEM((ITERS, CLASSES, top_rank), f32),
            sem((len(arrays),)),
            sem((n,)),
            sem((n,)),
            sem((ITERS, 2, n)),
            sem((ITERS, 2, n)),
            sem((ITERS, n)),
            sem((ITERS, n)),
            sem((ITERS, m)),
            sem((ITERS, m)),
            sem((ITERS, n)),
            sem((ITERS, n)),
        ],
        compiler_params=pltpu.CompilerParams(
            collective_id=0, has_side_effects=True, vmem_limit_bytes=48 * 1024 * 1024
        ),
    )(labels.reshape(1, rows), *arrays)
    dual_box = jnp.clip(moved, 0.0, 1.0)
    return (dual_box, moved - dual_box)


def solution(mesh):
    both = ("grp", "leaf")
    return jax.shard_map(
        functools.partial(shards, mesh.shape["leaf"], mesh.shape["grp"]),
        mesh=mesh,
        in_specs=(P(both),) + (P(both, None),) * 6 + (P("grp", None),),
        out_specs=(P(both, None), P(both, None)),
        check_vma=False,
    )
```

time: 149 us -> 61.9 us (0.42)
  blocking collectives: 79.3 us -> 0 us
  Pallas kernels: 0 us -> 52.1 us
  waiting for transfers between devices: 38.9 us -> 0 us
  between operations: 14.2 us -> 0.66 us
  matrix products: 11.5 us -> 0 us
  local copies, waits for them, and re-layouts: 4.27 us -> 7.69 us
    all_gather x6 -> x0, blocking collectives: 79.3 us -> none  [the longest x2 32.3 us: shards(): lax.all_gather(coeffs, 'leaf', axis=0, tiled=True)]
    pallas_call x0 -> x1, Pallas kernels: none -> 52.1 us  [shards(): pl.pallas_call(functools.partial(kernel, n, m), out_shape=jax.ShapeDtypeS...]
    reduce_scatter x2 -> x0, waiting for transfers between devices: 38.9 us -> none  [shards(): lax.psum_scatter(partial_proj, 'leaf', scatter_dimension=1, tiled=True)]
    dot_general x14 -> x0, matrix products: 11.5 us -> none  [the longest x10 7.88 us: matmul(): jnp.dot(left, right, precision=high, preferred_element_type=jnp.float32)]
    unnamed x22 -> x16, local copies, waits for them, and re-layouts: 4.27 us -> 7.69 us
  transfers between devices with their start and end apart: 2 -> 0, of which waited for: 2 -> 0; matrix products, arithmetic and copies ran while one was open for 0% -> 0% of each run, Pallas kernels for 0% -> 0%
where the time goes in v1:
time: 61.9 us; the launch traced here: 61.5 us
  Pallas kernels  52.1 us (84%)
  local copies, waits for them, and re-layouts  7.69 us (12%)
  other arithmetic  1.05 us (2%)
  between operations  0.66 us (1%)
    pallas_call x1, Pallas kernels, shards(): pl.pallas_call(functools.partial(kernel, n, m), out_shape=jax.ShapeDtypeS...  52.1 us
    unnamed x16, local copies, waits for them, and re-layouts  7.69 us

profile of v1, /device:TPU:0, one launch (start us, length us, event | category | flops | bytes accessed | tf_op | source)
XLA Modules:
  0.0 61.5 jit_solution(12210853675425568652)
XLA Ops:
  0.6 0.0 copy-start
  0.6 1.2 %copy-done = f32[512,512]{1,0:T(8,128)S(1)} copy-done((f32[512,512]{1,0:T(8,128)S(1)}, f32[512,512]{1,0:T(8,128)}, u32[]{:S(2)}) %copy-start) | copy-done | bytes 1048600
  1.9 0.0 copy-start.1
  1.9 1.0 %copy-done.1 = f32[128,1024]{1,0:T(8,128)S(1)} copy-done((f32[128,1024]{1,0:T(8,128)S(1)}, f32[128,1024]{1,0:T(8,128)}, u32[]{:S(2)}) %copy-start.1) | copy-done | bytes 524312
  2.9 0.0 copy-start.2
  2.9 0.9 %copy-done.2 = f32[512,128]{1,0:T(8,128)S(1)} copy-done((f32[512,128]{1,0:T(8,128)S(1)}, f32[512,128]{1,0:T(8,128)}, u32[]{:S(2)}) %copy-start.2) | copy-done | bytes 262168
  3.9 0.0 copy-start.3
  3.9 0.9 %copy-done.3 = f32[512,128]{1,0:T(8,128)S(1)} copy-done((f32[512,128]{1,0:T(8,128)S(1)}, f32[512,128]{1,0:T(8,128)}, u32[]{:S(2)}) %copy-start.3) | copy-done | bytes 262168
  4.8 0.0 copy-start.4
  4.8 0.9 %copy-done.4 = f32[128,512]{1,0:T(8,128)S(1)} copy-done((f32[128,512]{1,0:T(8,128)S(1)}, f32[128,512]{1,0:T(8,128)}, u32[]{:S(2)}) %copy-start.4) | copy-done | bytes 262168
  5.8 0.0 copy-start.5
  5.8 0.9 %copy-done.5 = f32[512,128]{1,0:T(8,128)S(1)} copy-done((f32[512,128]{1,0:T(8,128)S(1)}, f32[512,128]{1,0:T(8,128)}, u32[]{:S(2)}) %copy-start.5) | copy-done | bytes 262168
  6.7 0.0 copy-start.6
  6.7 0.9 %copy-done.6 = f32[512,128]{1,0:T(8,128)S(1)} copy-done((f32[512,128]{1,0:T(8,128)S(1)}, f32[512,128]{1,0:T(8,128)}, u32[]{:S(2)}) %copy-start.6) | copy-done | bytes 262168
  7.7 0.0 copy-start.7
  7.7 0.7 %copy-done.7 = s32[512]{0:T(512)S(1)} copy-done((s32[512]{0:T(512)S(1)}, s32[512]{0:T(512)}, u32[]{:S(2)}) %copy-start.7) | copy-done | bytes 2072
  8.3 52.1 %shard_map.95 = f32[512,256]{1,0:T(8,128)S(1)} custom-call(s32[1,512]{1,0:T(1,128)S(1)} %bitcast.1, f32[512,512]{1,0:T(8,128)S(1)} %copy-done, f32[512,128]{1,0:T(8,128)S(1)} %copy-done.2, f32[512,128]{1,0:T(8,128)S(1)} %copy-done.3, f32[128,512]{1,0:T(8,128)S(1)} %copy-done.4, f32[512,128]{1,0:T(8,128)S(1)} %copy-done.5, f32[512,128]{1,0:T(8,128)S(1)} %copy-done.6, ...), custom_call_target="tpu_custom_call" | custom-call | tf_op jit(solution)/shard_map/pallas_call | solution.py:289
  60.5 1.1 %fusion = (f32[512,256]{1,0:T(8,128)}, f32[512,256]{1,0:T(8,128)}) fusion(f32[512,256]{1,0:T(8,128)S(1)} %shard_map.95), kind=kLoop, calls=%fused_computation.1 | loop fusion | flops 262144 | bytes 1572864 | tf_op jit(solution)/shard_map/sub | solution.py:321
Async XLA Ops:
  0.6 1.2 %copy-start = (f32[512,512]{1,0:T(8,128)S(1)}, f32[512,512]{1,0:T(8,128)}, u32[]{:S(2)}) copy-start(f32[512,512]{1,0:T(8,128)} %inverse_hbm.1) | copy-start | bytes 3145732
  1.9 1.0 %copy-start.1 = (f32[128,1024]{1,0:T(8,128)S(1)}, f32[128,1024]{1,0:T(8,128)}, u32[]{:S(2)}) copy-start(f32[128,1024]{1,0:T(8,128)} %top_capacitance_hbm.1) | copy-start | bytes 1572868
  2.9 0.9 %copy-start.2 = (f32[512,128]{1,0:T(8,128)S(1)}, f32[512,128]{1,0:T(8,128)}, u32[]{:S(2)}) copy-start(f32[512,128]{1,0:T(8,128)} %basis_hbm.1) | copy-start | bytes 786436
  3.9 0.9 %copy-start.3 = (f32[512,128]{1,0:T(8,128)S(1)}, f32[512,128]{1,0:T(8,128)}, u32[]{:S(2)}) copy-start(f32[512,128]{1,0:T(8,128)} %solved_hbm.1) | copy-start | bytes 786436
  4.8 0.9 %copy-start.4 = (f32[128,512]{1,0:T(8,128)S(1)}, f32[128,512]{1,0:T(8,128)}, u32[]{:S(2)}) copy-start(f32[128,512]{1,0:T(8,128)} %capacitance_hbm.1) | copy-start | bytes 786436
  5.8 0.9 %copy-start.5 = (f32[512,128]{1,0:T(8,128)S(1)}, f32[512,128]{1,0:T(8,128)}, u32[]{:S(2)}) copy-start(f32[512,128]{1,0:T(8,128)} %top_basis_hbm.1) | copy-start | bytes 786436
  6.7 0.9 %copy-start.6 = (f32[512,128]{1,0:T(8,128)S(1)}, f32[512,128]{1,0:T(8,128)}, u32[]{:S(2)}) copy-start(f32[512,128]{1,0:T(8,128)} %top_solved_hbm.1) | copy-start | bytes 786436
  7.7 0.7 %copy-start.7 = (s32[512]{0:T(512)S(1)}, s32[512]{0:T(512)}, u32[]{:S(2)}) copy-start(s32[512]{0:T(512)} %param.8) | copy-start | bytes 6148

commit v2 on v1

v2 whole, which is shorter than its diff:
```python
import functools

import jax
import jax.numpy as jnp
from jax import lax
from jax.experimental import pallas as pl
from jax.experimental.pallas import tpu as pltpu
from jax.sharding import PartitionSpec as P

CLASSES = 256
ITERS = 2
CHUNKS = 2
WIDTH = CLASSES // CHUNKS
UNITS = ITERS * CHUNKS
NN = (((1,), (0,)), ((), ()))
NT = (((1,), (1,)), ((), ()))


def split(x):
    high = x.astype(jnp.bfloat16)
    low = (x - high.astype(jnp.float32)).astype(jnp.bfloat16)
    return high, low


def dot(a, b, dims):
    return lax.dot_general(a, b, dims, preferred_element_type=jnp.float32)


def product(a, b, dims=NN):
    return dot(a[0], b[0], dims) + (dot(a[0], b[1], dims) + dot(a[1], b[0], dims))


def kernel(
    n,
    m,
    labels_ref,
    inverse_hbm,
    basis_hbm,
    solved_hbm,
    capacitance_hbm,
    top_basis_hbm,
    top_solved_hbm,
    top_capacitance_hbm,
    moved_ref,
    inverse_ref,
    basis_ref,
    solved_ref,
    capacitance_ref,
    top_basis_ref,
    top_solved_ref,
    top_capacitance_ref,
    w_out,
    w_in,
    c_all,
    p_out,
    p_in,
    proj,
    t_all,
    in_sem,
    w_send,
    w_recv,
    c_send,
    c_recv,
    p_send,
    p_recv,
    g_send,
    g_recv,
    t_send,
    t_recv,
):
    me = lax.axis_index("leaf")
    grp = lax.axis_index("grp")
    rows = labels_ref.shape[1]
    rank = basis_ref.shape[1]
    top_rank = top_basis_ref.shape[1]
    share = WIDTH // n

    sources = (
        (inverse_hbm, inverse_ref),
        (basis_hbm, basis_ref),
        (capacitance_hbm, capacitance_ref),
        (solved_hbm, solved_ref),
        (top_basis_hbm, top_basis_ref),
        (top_solved_hbm, top_solved_ref),
        (top_capacitance_hbm, top_capacitance_ref),
    )
    loads = [pltpu.make_async_copy(a, b, in_sem.at[i]) for i, (a, b) in enumerate(sources)]
    for i in (4, 3, 2, 0, 1, 5, 6):
        loads[i].start()

    barrier = pltpu.get_barrier_semaphore()
    for d in range(1, n):
        pl.semaphore_signal(
            barrier, inc=1, device_id={"leaf": lax.rem(me + d, n)},
            device_id_type=pl.DeviceIdType.MESH,
        )
    for d in range(1, m):
        pl.semaphore_signal(
            barrier, inc=1, device_id={"grp": lax.rem(grp + d, m)},
            device_id_type=pl.DeviceIdType.MESH,
        )

    def remote(src, dst, send, recv, where):
        return pltpu.make_async_remote_copy(
            src_ref=src, dst_ref=dst, send_sem=send, recv_sem=recv,
            device_id=where, device_id_type=pl.DeviceIdType.MESH,
        )

    sent = []

    pieces = []
    for r in range(rows // 128):
        row = labels_ref[:, r * 128 : (r + 1) * 128].astype(jnp.float32)
        column = jnp.broadcast_to(row, (128, 128)).T
        lanes = lax.broadcasted_iota(jnp.int32, (128, 128), 1)
        pieces.append(
            jnp.concatenate(
                [
                    jnp.where(column == (lanes + k * 128).astype(jnp.float32), 1.0, -1.0)
                    for k in range(CLASSES // 128)
                ],
                axis=1,
            )
        )
    sign = jnp.concatenate(pieces, axis=0)

    mine = pl.ds(pl.multiple_of(me * share, 8), share)
    state = [{} for _ in range(UNITS)]

    def begin(u):
        st, chunk = state[u], u % CHUNKS
        st["sign"] = sign[:, chunk * WIDTH : (chunk + 1) * WIDTH]
        if u < CHUNKS:
            exact = st["sign"].astype(jnp.bfloat16)
            st["local"] = dot(inverse[0], exact, NN) + dot(inverse[1], exact, NN)
        else:
            prev = state[u - CHUNKS]
            rhs = st["sign"] * (1.0 + 1.0 * (prev["dual_box"] - prev["scaled_dual"]))
            st["local"] = product(inverse, split(rhs))

    def send_p(u, partial):
        p_out[u] = partial.T
        for d in range(1, n):
            dest = lax.rem(me + d, n)
            copy = remote(
                p_out.at[u, pl.ds(pl.multiple_of(dest * share, 8), share)],
                p_in.at[u, d], p_send.at[u, d], p_recv.at[u, d], {"leaf": dest},
            )
            copy.start()
            sent.append((None, copy))

    def step(u, k):
        left, right = jnp.maximum(me - k, 0), jnp.minimum(me + k, n - 1)
        has_left, has_right = me - k >= 0, me + k <= n - 1
        for side, src, has, more, dest in (
            (0, left, has_left, me < n - 1, jnp.minimum(me + 1, n - 1)),
            (1, right, has_right, me > 0, jnp.maximum(me - 1, 0)),
        ):
            if k:
                @pl.when(has)
                def _(src=src, side=side):
                    remote(
                        c_all.at[u, src], c_all.at[u, src], c_send.at[u, side, k],
                        c_recv.at[u, side, k], {"leaf": me},
                    ).wait_recv()
            if k < n - 1:
                copy = remote(
                    c_all.at[u, src], c_all.at[u, src], c_send.at[u, side, k],
                    c_recv.at[u, side, k + 1], {"leaf": dest},
                )

                @pl.when(has & more)
                def _(copy=copy):
                    copy.start()

                sent.append((has & more, copy))

    def correct(u):
        st = state[u]
        coeffs = jnp.concatenate([c_all[u, k] for k in range(n)], axis=0)
        group_coef = product(capacitance, split(coeffs))
        st["inner"] = st["local"] - product(solved, split(group_coef))

    def gather(u):
        total = p_out[u, mine]
        for d in range(1, n):
            remote(
                p_in.at[u, 0], p_in.at[u, d], p_send.at[u, d], p_recv.at[u, d], {"leaf": me}
            ).wait_recv()
            total = total + p_in[u, d]
        proj[u, grp] = total
        for d in range(1, m):
            copy = remote(
                proj.at[u, grp], proj.at[u, grp], g_send.at[u, d], g_recv.at[u, d],
                {"grp": lax.rem(grp + d, m)},
            )
            copy.start()
            sent.append((None, copy))

    def top(u):
        for d in range(1, m):
            src = lax.rem(grp + m - d, m)
            remote(
                proj.at[u, src], proj.at[u, src], g_send.at[u, d], g_recv.at[u, d], {"grp": grp}
            ).wait_recv()
        stacked = jnp.concatenate([proj[u, g] for g in range(m)], axis=1)
        t_all[u, mine] = product(split(stacked), top_capacitance, NT)
        for d in range(1, n):
            copy = remote(
                t_all.at[u, mine], t_all.at[u, mine], t_send.at[u, d], t_recv.at[u, d],
                {"leaf": lax.rem(me + d, n)},
            )
            copy.start()
            sent.append((None, copy))

    def finish(u):
        st, chunk = state[u], u % CHUNKS
        for d in range(1, n):
            src = pl.ds(pl.multiple_of(lax.rem(me + n - d, n) * share, 8), share)
            remote(
                t_all.at[u, src], t_all.at[u, src], t_send.at[u, d], t_recv.at[u, d], {"leaf": me}
            ).wait_recv()
        moved = st["sign"] * (st["inner"] - product(top_solved, split(t_all[u]), NT))
        if u >= CHUNKS:
            moved = state[u - CHUNKS]["scaled_dual"] + moved
        if u < UNITS - CHUNKS:
            st["dual_box"] = jnp.clip(moved, 0.0, 1.0)
            st["scaled_dual"] = moved - st["dual_box"]
        else:
            moved_ref[:, chunk * WIDTH : (chunk + 1) * WIDTH] = moved

    for i in (2, 3, 4):
        loads[i].wait()
    top_basis_t = top_basis_ref[...].T
    solved = split(solved_ref[...])
    capacitance = split(capacitance_ref[...])
    coupling = product(split(product(split(top_basis_t), solved)), capacitance)
    for d in range(n):
        w_out[d] = coupling[:, d * rank : (d + 1) * rank]
    pl.semaphore_wait(barrier, n - 1 + m - 1)
    for d in range(1, n):
        dest = lax.rem(me + d, n)
        copy = remote(w_out.at[dest], w_in.at[d], w_send.at[d], w_recv.at[d], {"leaf": dest})
        copy.start()
        sent.append((None, copy))
    loads[0].wait()
    inverse = split(inverse_ref[...])
    for u in range(CHUNKS):
        begin(u)
    loads[1].wait()
    loads[5].wait()
    loads[6].wait()
    basis_t = basis_ref[...].T
    top_solved = split(top_solved_ref[...])
    top_capacitance = split(top_capacitance_ref[...])
    w_sum = w_out[me]
    for d in range(1, n):
        remote(w_out.at[0], w_in.at[d], w_send.at[d], w_recv.at[d], {"leaf": me}).wait_recv()
        w_sum = w_sum + w_in[d]
    combined = top_basis_t - product(split(w_sum), split(basis_ref[...]), NT)
    projector = split(jnp.concatenate([basis_t, combined], axis=0))
    for it in range(ITERS):
        units = range(it * CHUNKS, (it + 1) * CHUNKS)
        for u in units:
            if it:
                finish(u - CHUNKS)
                begin(u)
            both = product(projector, split(state[u]["local"]))
            send_p(u, both[rank:, :])
            c_all[u, me] = both[:rank, :]
        for u in units:
            step(u, 0)
        for u in units:
            gather(u)
        for u in units:
            step(u, 1)
        for u in units:
            top(u)
        for k in range(2, n):
            for u in units:
                step(u, k)
        for u in units:
            correct(u)
    for u in range(UNITS - CHUNKS, UNITS):
        finish(u)
    for has, copy in sent:
        if has is None:
            copy.wait_send()
        else:
            @pl.when(has)
            def _(copy=copy):
                copy.wait_send()


def shards(
    n,
    m,
    labels,
    leaf_inverse,
    leaf_basis,
    leaf_solved,
    group_capacitance,
    top_basis,
    top_solved,
    top_capacitance,
):
    rows = labels.shape[0]
    rank = leaf_basis.shape[1]
    top_rank = top_basis.shape[1]
    share = WIDTH // n
    arrays = (
        leaf_inverse,
        leaf_basis,
        leaf_solved,
        group_capacitance,
        top_basis,
        top_solved,
        top_capacitance,
    )
    f32 = jnp.float32
    sem = pltpu.SemaphoreType.DMA
    moved = pl.pallas_call(
        functools.partial(kernel, n, m),
        out_shape=jax.ShapeDtypeStruct((rows, CLASSES), f32),
        in_specs=[pl.BlockSpec(memory_space=pltpu.VMEM)]
        + [pl.BlockSpec(memory_space=pltpu.HBM)] * len(arrays),
        out_specs=pl.BlockSpec(memory_space=pltpu.VMEM),
        scratch_shapes=[pltpu.VMEM(a.shape, f32) for a in arrays]
        + [
            pltpu.VMEM((n, top_rank, rank), f32),
            pltpu.VMEM((n, top_rank, rank), f32),
            pltpu.VMEM((UNITS, n, rank, WIDTH), f32),
            pltpu.VMEM((UNITS, WIDTH, top_rank), f32),
            pltpu.VMEM((UNITS, n, share, top_rank), f32),
            pltpu.VMEM((UNITS, m, share, top_rank), f32),
            pltpu.VMEM((UNITS, WIDTH, top_rank), f32),
            sem((len(arrays),)),
            sem((n,)),
            sem((n,)),
            sem((UNITS, 2, n)),
            sem((UNITS, 2, n)),
            sem((UNITS, n)),
            sem((UNITS, n)),
            sem((UNITS, m)),
            sem((UNITS, m)),
            sem((UNITS, n)),
            sem((UNITS, n)),
        ],
        compiler_params=pltpu.CompilerParams(
            collective_id=0, has_side_effects=True, vmem_limit_bytes=62 * 1024 * 1024
        ),
    )(labels.reshape(1, rows), *arrays)
    dual_box = jnp.clip(moved, 0.0, 1.0)
    return (dual_box, moved - dual_box)


def solution(mesh):
    both = ("grp", "leaf")
    return jax.shard_map(
        functools.partial(shards, mesh.shape["leaf"], mesh.shape["grp"]),
        mesh=mesh,
        in_specs=(P(both),) + (P(both, None),) * 6 + (P("grp", None),),
        out_specs=(P(both, None), P(both, None)),
        check_vma=False,
    )
```

time: 61.9 us -> 54.6 us (0.88)
  local copies, waits for them, and re-layouts: 7.69 us -> 0 us
  other arithmetic: 1.05 us -> 2.1 us
    unnamed x16 -> x0, local copies, waits for them, and re-layouts: 7.69 us -> none
    sub x1, other arithmetic: 1.05 us -> 2.1 us  [shards(): return (dual_box, moved - dual_box)]
where the time goes in v2:
time: 54.6 us; the launch traced here: 54.3 us
  Pallas kernels  51.6 us (95%)
  other arithmetic  2.1 us (4%)
  between operations  0.64 us (1%)
    pallas_call x1, Pallas kernels, shards(): pl.pallas_call(functools.partial(kernel, n, m), out_shape=jax.ShapeDtypeS...  51.6 us
    sub x1, other arithmetic, shards(): return (dual_box, moved - dual_box)  2.1 us

profile of v2, /device:TPU:0, one launch (start us, length us, event | category | flops | bytes accessed | tf_op | source)
XLA Modules:
  0.0 54.3 jit_solution(9539636582837225763)
XLA Ops:
  0.6 51.6 %shard_map.95 = f32[512,256]{1,0:T(8,128)} custom-call(s32[1,512]{1,0:T(1,128)} %bitcast.1, f32[512,512]{1,0:T(8,128)} %inverse_hbm.1, f32[512,128]{1,0:T(8,128)} %basis_hbm.1, f32[512,128]{1,0:T(8,128)} %solved_hbm.1, f32[128,512]{1,0:T(8,128)} %capacitance_hbm.1, f32[512,128]{1,0:T(8,128)} %top_basis_hbm.1, f32[512,128]{1,0:T(8,128)} %top_solved_hbm.1, ...), custom_call_target="tpu_custom_call" | custom-call | tf_op jit(solution)/shard_map/pallas_call | solution.py:322
  52.2 2.1 %fusion = (f32[512,256]{1,0:T(8,128)}, f32[512,256]{1,0:T(8,128)}) fusion(f32[512,256]{1,0:T(8,128)} %shard_map.95), kind=kLoop, calls=%fused_computation.1 | loop fusion | flops 262144 | bytes 1572864 | tf_op jit(solution)/shard_map/sub | solution.py:354
